TPU v7x, 32 devices: a whole 2x2x4 slice. The times are simulated.
32 devices in a mesh: rep: 8 (over z, y), fsdp: 2 (over x), ctx: 2 (over core).
Axes of the slice: x: 2, y: 2, z: 4, core: 2. Of those that a mesh axis runs over, the one named last changes fastest.
Arguments:
- tokens: bfloat16 [32, 1024, 1280], P(('rep', 'fsdp'), 'ctx'), may hold values from -6 to 6
- prefixes: int32 [32], P(('rep', 'fsdp')), may hold values from 102 to 512, as said below
- query_weight: bfloat16 [1280, 1280], P(('fsdp', 'ctx')), may hold values from -0.15625 to 0.15625
- key_weight: bfloat16 [1280, 1280], P(('fsdp', 'ctx')), may hold values from -0.15625 to 0.15625
- value_weight: bfloat16 [1280, 1280], P(('fsdp', 'ctx')), may hold values from -0.15625 to 0.15625
- output_weight: bfloat16 [1280, 1280], P(('fsdp', 'ctx')), may hold values from -2 to 2
- up_weight: bfloat16 [1280, 1280], P(('fsdp', 'ctx')), may hold values from -0.15625 to 0.15625
- up_bias: float32 [1280], replicated, may hold values from -3 to 3
- down_weight: bfloat16 [1280, 1280], P(('fsdp', 'ctx')), may hold values from -0.15625 to 0.15625
- down_bias: float32 [1280], replicated, may hold values from -3 to 3
- attn_gain: float32 [1280], replicated, may hold values from 0.5 to 1.5
- mlp_gain: float32 [1280], replicated, may hold values from 0.5 to 1.5
- query_scale: float32 [80], replicated, may hold values from -2.5 to 2.5
- cotangent: bfloat16 [32, 1024, 1280], P(('rep', 'fsdp'), 'ctx'), may hold values from -6 to 6
Outputs:
- mixed: bfloat16 [32, 1024, 1280], P(('rep', 'fsdp'), 'ctx')
- tokens_grad: bfloat16 [32, 1024, 1280], P(('rep', 'fsdp'), 'ctx')
- query_grad: float32 [1280, 1280], P(('fsdp', 'ctx'))
- key_grad: float32 [1280, 1280], P(('fsdp', 'ctx'))
- value_grad: float32 [1280, 1280], P(('fsdp', 'ctx'))
- output_grad: float32 [1280, 1280], P(('fsdp', 'ctx'))
- up_grad: float32 [1280, 1280], P(('fsdp', 'ctx'))
- upbias_grad: float32 [1280], replicated
- down_grad: float32 [1280, 1280], P(('fsdp', 'ctx'))
- downbias_grad: float32 [1280], replicated
- attngain_grad: float32 [1280], replicated
- mlpgain_grad: float32 [1280], replicated
- scale_grad: float32 [80], replicated
Inputs may be any that keep to these rules, and one draw needn't show every extreme that they name: `prefixes`: at least one sequence has 1024 // 10 and one has 1024 // 2.
All inputs are finite; a program needn't handle non-finite values.
Results may differ from a plain program's by a relative error of at most 0.02.
Values may be sent and summed in bfloat16 or wider, within the bound.
No kernel may reach another device: no remote copies, remote signals or barrier semaphores. Data moves between devices by JAX's collectives and lax.ppermute only.
A program may use at most 384 MiB of HBM per device.

v0:
```python
import jax
import jax.numpy as jnp
from jax import lax
from jax.sharding import PartitionSpec as P

HD = 80
epsilon = 1e-06
softplus_gain = 1.442695041
masked_value = -1e30


def norm_factor(values):
    return lax.rsqrt(jnp.mean(values * values, axis=-1, keepdims=True) + epsilon)


def norm_back(upstream, values, factor, gain_vec):
    scaled = upstream * gain_vec
    row_inner = jnp.mean(scaled * values, axis=-1, keepdims=True)
    return factor * scaled - values * factor**3 * row_inner


def allowed_mask(offset, local_rows, length, prefix):
    row_index = offset + jnp.arange(local_rows, dtype=jnp.int32)[:, None]
    col_index = jnp.arange(length, dtype=jnp.int32)[None, :]
    return (col_index <= row_index) | (col_index < prefix)


def masked_scores(queries, keys, allowed):
    scores = jnp.einsum("qhe,khe->hqk", queries, keys, preferred_element_type=jnp.float32)
    return jnp.where(allowed[None], scores, masked_value)


def shards(
    tokens,
    prefixes,
    query_weight,
    key_weight,
    value_weight,
    output_weight,
    up_weight,
    up_bias,
    down_weight,
    down_bias,
    attn_gain,
    mlp_gain,
    query_scale,
    cotangent,
):
    seq_count, local_rows, model_width = tokens.shape
    head_count = model_width // HD
    position_index = lax.axis_index("ctx")
    offset = position_index * local_rows
    full_query, full_key, full_value, full_output, full_up, full_down = (
        lax.all_gather(query_weight, ("fsdp", "ctx"), axis=0, tiled=True),
        lax.all_gather(key_weight, ("fsdp", "ctx"), axis=0, tiled=True),
        lax.all_gather(value_weight, ("fsdp", "ctx"), axis=0, tiled=True),
        lax.all_gather(output_weight, ("fsdp", "ctx"), axis=0, tiled=True),
        lax.all_gather(up_weight, ("fsdp", "ctx"), axis=0, tiled=True),
        lax.all_gather(down_weight, ("fsdp", "ctx"), axis=0, tiled=True),
    )
    rows_in = tokens.reshape(seq_count * local_rows, model_width).astype(jnp.float32)
    factor_one = norm_factor(rows_in)
    normed = (rows_in * factor_one * attn_gain).astype(jnp.bfloat16)
    scale_soft = jax.nn.softplus(query_scale) * (softplus_gain * HD ** (-0.5))
    query_raw = jnp.dot(normed, full_query, preferred_element_type=jnp.float32).reshape(
        seq_count, local_rows, head_count, HD
    )
    queries = (query_raw * scale_soft).astype(jnp.bfloat16)
    key_local = (
        jnp.dot(normed, full_key, preferred_element_type=jnp.float32)
        .astype(jnp.bfloat16)
        .reshape(seq_count, local_rows, model_width)
    )
    value_local = (
        jnp.dot(normed, full_value, preferred_element_type=jnp.float32)
        .astype(jnp.bfloat16)
        .reshape(seq_count, local_rows, model_width)
    )
    key_all, value_all = (
        lax.all_gather(key_local, "ctx", axis=1, tiled=True),
        lax.all_gather(value_local, "ctx", axis=1, tiled=True),
    )
    length = key_all.shape[1]

    def forward_one(members):
        queries_seq, keys_seq, values_seq, prefix = members
        allowed = allowed_mask(offset, local_rows, length, prefix)
        scores = masked_scores(queries_seq, keys_seq.reshape(length, head_count, HD), allowed)
        row_max = jnp.max(scores, axis=-1, keepdims=True)
        weights = jnp.exp(scores - row_max)
        row_total = jnp.sum(weights, axis=-1, keepdims=True)
        probability = (weights / row_total).astype(jnp.bfloat16)
        context = jnp.einsum(
            "hqk,khe->qhe",
            probability,
            values_seq.reshape(length, head_count, HD),
            preferred_element_type=jnp.float32,
        )
        return (context, row_max + jnp.log(row_total))

    context, logsum = lax.map(forward_one, (queries, key_all, value_all, prefixes))
    attended = context.reshape(seq_count * local_rows, model_width).astype(jnp.bfloat16)
    middle = rows_in + jnp.dot(attended, full_output, preferred_element_type=jnp.float32)
    factor_two = norm_factor(middle)
    normed_two = (middle * factor_two * mlp_gain).astype(jnp.bfloat16)
    before = jnp.dot(normed_two, full_up, preferred_element_type=jnp.float32) + up_bias
    hidden = jax.nn.silu(before).astype(jnp.bfloat16)
    mixed_rows = middle + jnp.dot(hidden, full_down, preferred_element_type=jnp.float32) + down_bias
    mixed_out = mixed_rows.astype(jnp.bfloat16).reshape(seq_count, local_rows, model_width)
    key_back, value_back = (key_all, value_all)
    back_query, back_key, back_value, back_output, back_up, back_down = (
        lax.all_gather(query_weight, ("fsdp", "ctx"), axis=0, tiled=True),
        lax.all_gather(key_weight, ("fsdp", "ctx"), axis=0, tiled=True),
        lax.all_gather(value_weight, ("fsdp", "ctx"), axis=0, tiled=True),
        lax.all_gather(output_weight, ("fsdp", "ctx"), axis=0, tiled=True),
        lax.all_gather(up_weight, ("fsdp", "ctx"), axis=0, tiled=True),
        lax.all_gather(down_weight, ("fsdp", "ctx"), axis=0, tiled=True),
    )
    key_back, value_back = (
        lax.all_gather(key_local, "ctx", axis=1, tiled=True),
        lax.all_gather(value_local, "ctx", axis=1, tiled=True),
    )
    upstream = cotangent.reshape(seq_count * local_rows, model_width)
    upstream_wide = upstream.astype(jnp.float32)
    down_part = jnp.einsum("nf,nd->fd", hidden, upstream, preferred_element_type=jnp.float32)
    downbias_part = jnp.sum(upstream_wide, axis=0)
    hidden_grad = jnp.einsum("nd,fd->nf", upstream, back_down, preferred_element_type=jnp.float32)
    gate_sig = jax.nn.sigmoid(before)
    before_grad = (hidden_grad * gate_sig * (1.0 + before * (1.0 - gate_sig))).astype(jnp.bfloat16)
    up_part = jnp.einsum("nd,nf->df", normed_two, before_grad, preferred_element_type=jnp.float32)
    upbias_part = jnp.sum(before_grad.astype(jnp.float32), axis=0)
    normed_grad = jnp.einsum("nf,df->nd", before_grad, back_up, preferred_element_type=jnp.float32)
    mlpgain_part = jnp.sum(normed_grad * middle * factor_two, axis=0)
    middle_grad = upstream_wide + norm_back(normed_grad, middle, factor_two, mlp_gain)
    middle_low = middle_grad.astype(jnp.bfloat16)
    output_part = jnp.einsum("nd,ne->de", attended, middle_low, preferred_element_type=jnp.float32)
    context_grad = jnp.einsum(
        "ne,de->nd", middle_low, back_output, preferred_element_type=jnp.float32
    )
    context_grad = context_grad.astype(jnp.bfloat16).reshape(seq_count, local_rows, head_count, HD)

    def backward_one(members):
        queries_seq, keys_seq, values_seq, grad_seq, logsum_seq, prefix = members
        keys_heads = keys_seq.reshape(length, head_count, HD)
        values_heads = values_seq.reshape(length, head_count, HD)
        allowed = allowed_mask(offset, local_rows, length, prefix)
        scores = masked_scores(queries_seq, keys_heads, allowed)
        exact_prob = jnp.exp(scores - logsum_seq)
        probability = exact_prob.astype(jnp.bfloat16)
        prob_grad = jnp.einsum(
            "qhe,khe->hqk", grad_seq, values_heads, preferred_element_type=jnp.float32
        )
        row_inner = jnp.sum(prob_grad * exact_prob, axis=-1, keepdims=True)
        score_grad = (exact_prob * (prob_grad - row_inner)).astype(jnp.bfloat16)
        query_part = jnp.einsum(
            "hqk,khe->qhe", score_grad, keys_heads, preferred_element_type=jnp.float32
        )
        key_term = jnp.einsum(
            "hqk,qhe->khe", score_grad, queries_seq, preferred_element_type=jnp.float32
        )
        value_term = jnp.einsum(
            "hqk,qhe->khe", probability, grad_seq, preferred_element_type=jnp.float32
        )
        return (
            query_part,
            key_term.reshape(length, model_width),
            value_term.reshape(length, model_width),
        )

    query_seqgrad, key_partial, value_partial = lax.map(
        backward_one, (queries, key_back, value_back, context_grad, logsum, prefixes)
    )
    key_summed, value_summed = (
        lax.psum_scatter(key_partial, "ctx", scatter_dimension=1, tiled=True),
        lax.psum_scatter(value_partial, "ctx", scatter_dimension=1, tiled=True),
    )
    key_low = key_summed.astype(jnp.bfloat16).reshape(seq_count * local_rows, model_width)
    value_low = value_summed.astype(jnp.bfloat16).reshape(seq_count * local_rows, model_width)
    scaled_low = query_seqgrad.astype(jnp.bfloat16)
    query_low = (
        (scaled_low * scale_soft).astype(jnp.bfloat16).reshape(seq_count * local_rows, model_width)
    )
    scale_part = jnp.sum(scaled_low * query_raw, axis=(0, 1, 2))
    scale_part = scale_part * jax.nn.sigmoid(query_scale) * (softplus_gain * HD ** (-0.5))
    query_part = jnp.einsum("nd,ne->de", normed, query_low, preferred_element_type=jnp.float32)
    key_part = jnp.einsum("nd,ne->de", normed, key_low, preferred_element_type=jnp.float32)
    value_part = jnp.einsum("nd,ne->de", normed, value_low, preferred_element_type=jnp.float32)
    normed_grad_one = jnp.einsum(
        "ne,de->nd", query_low, back_query, preferred_element_type=jnp.float32
    )
    normed_grad_one = normed_grad_one + jnp.einsum(
        "ne,de->nd", key_low, back_key, preferred_element_type=jnp.float32
    )
    normed_grad_one = normed_grad_one + jnp.einsum(
        "ne,de->nd", value_low, back_value, preferred_element_type=jnp.float32
    )
    attngain_part = jnp.sum(normed_grad_one * rows_in * factor_one, axis=0)
    tokens_grad = middle_grad + norm_back(normed_grad_one, rows_in, factor_one, attn_gain)
    tokens_grad = tokens_grad.astype(jnp.bfloat16).reshape(seq_count, local_rows, model_width)
    query_shard, key_shard, value_shard, output_shard, up_shard, down_shard = (
        lax.psum_scatter(
            query_part.astype(jnp.bfloat16), ("fsdp", "ctx"), scatter_dimension=0, tiled=True
        ).astype(jnp.float32),
        lax.psum_scatter(
            key_part.astype(jnp.bfloat16), ("fsdp", "ctx"), scatter_dimension=0, tiled=True
        ).astype(jnp.float32),
        lax.psum_scatter(
            value_part.astype(jnp.bfloat16), ("fsdp", "ctx"), scatter_dimension=0, tiled=True
        ).astype(jnp.float32),
        lax.psum_scatter(
            output_part.astype(jnp.bfloat16), ("fsdp", "ctx"), scatter_dimension=0, tiled=True
        ).astype(jnp.float32),
        lax.psum_scatter(
            up_part.astype(jnp.bfloat16), ("fsdp", "ctx"), scatter_dimension=0, tiled=True
        ).astype(jnp.float32),
        lax.psum_scatter(
            down_part.astype(jnp.bfloat16), ("fsdp", "ctx"), scatter_dimension=0, tiled=True
        ).astype(jnp.float32),
    )
    query_total, key_total, value_total, output_total, up_total, down_total = (
        lax.psum(query_shard.astype(jnp.bfloat16), "rep").astype(jnp.float32),
        lax.psum(key_shard.astype(jnp.bfloat16), "rep").astype(jnp.float32),
        lax.psum(value_shard.astype(jnp.bfloat16), "rep").astype(jnp.float32),
        lax.psum(output_shard.astype(jnp.bfloat16), "rep").astype(jnp.float32),
        lax.psum(up_shard.astype(jnp.bfloat16), "rep").astype(jnp.float32),
        lax.psum(down_shard.astype(jnp.bfloat16), "rep").astype(jnp.float32),
    )
    upbias_total, downbias_total, attngain_total, mlpgain_total, scale_total = lax.psum(
        (upbias_part, downbias_part, attngain_part, mlpgain_part, scale_part),
        ("rep", "fsdp", "ctx"),
    )
    return (
        mixed_out,
        tokens_grad,
        query_total,
        key_total,
        value_total,
        output_total,
        up_total,
        upbias_total,
        down_total,
        downbias_total,
        attngain_total,
        mlpgain_total,
        scale_total,
    )


def solution(mesh):
    return jax.shard_map(
        shards,
        mesh=mesh,
        in_specs=(
            P(("rep", "fsdp"), "ctx", None),
            P(("rep", "fsdp")),
            P(("fsdp", "ctx"), None),
            P(("fsdp", "ctx"), None),
            P(("fsdp", "ctx"), None),
            P(("fsdp", "ctx"), None),
            P(("fsdp", "ctx"), None),
            P(),
            P(("fsdp", "ctx"), None),
            P(),
            P(),
            P(),
            P(),
            P(("rep", "fsdp"), "ctx", None),
        ),
        out_specs=(
            P(("rep", "fsdp"), "ctx", None),
            P(("rep", "fsdp"), "ctx", None),
            P(("fsdp", "ctx"), None),
            P(("fsdp", "ctx"), None),
            P(("fsdp", "ctx"), None),
            P(("fsdp", "ctx"), None),
            P(("fsdp", "ctx"), None),
            P(),
            P(("fsdp", "ctx"), None),
            P(),
            P(),
            P(),
            P(),
        ),
        check_vma=False,
    )
```

profile of v0, /device:TPU:0, one launch (start us, length us, event | category | flops | bytes accessed | tf_op | source)
XLA Modules:
  0.0 1070.1 jit_solution(11149948379400811405)
XLA Ops:
  15.3 26.3 %all-gather.15.cloned.1.call-done = bf16[1280,1280]{1,0:T(8,128)(2,1)} async-done(((bf16[320,1280]{1,0:T(8,128)(2,1)}), bf16[1280,1280]{1,0:T(8,128)(2,1)}) %all-gather.15.cloned.1.call-update) | async-done | bytes 3276816 | tf_op jit(solution)/shard_map/all_gather | solution.py:55
  41.6 7.8 convolution_convert_fusion.5
  49.3 4.5 copy.37
  53.9 18.5 %all-gather.9.cloned.1.call-done = bf16[1280,1280]{1,0:T(8,128)(2,1)} async-done(((bf16[320,1280]{1,0:T(8,128)(2,1)}), bf16[1280,1280]{1,0:T(8,128)(2,1)}) %all-gather.9.cloned.1.call-update) | async-done | bytes 3276816 | tf_op jit(solution)/shard_map/all_gather | solution.py:56
  72.4 7.8 convolution_convert_fusion.6
  80.2 4.5 copy.35
  89.3 14.0 %all-gather.13.cloned.1.call-done = bf16[1280,1280]{1,0:T(8,128)(2,1)} async-done(((bf16[320,1280]{1,0:T(8,128)(2,1)}), bf16[1280,1280]{1,0:T(8,128)(2,1)}) %all-gather.13.cloned.1.call-update) | async-done | bytes 3276816 | tf_op jit(solution)/shard_map/all_gather | solution.py:54
  103.3 5.6 copy.36
  108.9 9.2 multiply_convert_fusion.4
  119.9 18.4 %all-gather.11.cloned.1.call-done = bf16[2,1024,1280]{1,2,0:T(8,128)(2,1)} async-done(((bf16[2,512,1280]{1,2,0:T(8,128)(2,1)}), bf16[2,1024,1280]{1,2,0:T(8,128)(2,1)}) %all-gather.11.cloned.1.call-update) | async-done | bytes 5242896 | tf_op jit(solution)/shard_map/all_gather | solution.py:81
  140.1 103.8 %while.26 = (s32[]{:T(128)}, bf16[2,512,16,80]{1,3,2,0:T(8,128)(2,1)}, f32[2,16,512,1]{2,1,3,0:T(8,128)S(1)}, bf16[2,1024,1280]{1,2,0:T(8,128)(2,1)}, s32[]{:T(1...) while((s32[]{:T(128)}, ...), condition=%wide.region_4.5_spmd, body=%wide.region_1.4_spmd.sunk | while | flops 2760893952 | bytes 154147024 | solution.py:101
  141.7 4.6 constant_dynamic-slice_fusion.7
  146.4 13.5 %select_reduce_fusion.2 = (f32[16,512]{1,0:T(8,128)S(1)}, f32[16,512,1024]{2,1,0:T(8,128)}) fusion(pred[512,1024]{1,0:T(8,128)(4,1)S(1)} %fusion.112, bf16[1024,16,80]{0,2,1:T(8,128)(2,1)S(1)} %bitcast.193, bf16[2,512,16,80]{1,3,2,0:T(8,128)(2,1)S(1)} %get-tuple-element.373, s32[]{:T(128)S(6)} %copy.79), kind=kOutput, calls=%fused_computation.2.clone.1 | convolution fusion | flops 1358946304 | bytes 38043652 | tf_op jit(solution)/shard_map/while/body/eval_jaxpr/qhe,khe->hqk/dot_general | solution.py:29
  159.9 15.4 %fusion.113 = f32[16,512]{1,0:T(8,128)S(1)} fusion(f32[16,512,1024]{2,1,0:T(8,128)} %get-tuple-element.332, f32[16,512]{1,0:T(8,128)S(1)} %get-tuple-element.333, pred[512,1024]{1,0:T(8,128)(4,1)S(1)} %fusion.112), kind=kLoop, calls=%fused_computation.3.clone.1 | loop fusion | flops 25157632 | bytes 34144256 | tf_op jit(solution)/shard_map/while/body/eval_jaxpr/reduce_sum | solution.py:91
  175.3 15.2 %bitcast_dynamic-update-slice_fusion.6 = bf16[2,512,16,80]{1,3,2,0:T(8,128)(2,1)S(1)} fusion(bf16[2,512,16,80]{1,3,2,0:T(8,128)(2,1)S(1)} %copy-done.8, s32[]{:T(128)S(6)} %copy.79, bf16[1024,16,80]{0,2,1:T(8,128)(2,1)S(1)} %bitcast.196, f32[16,512,1024]{2,1,0:T(8,128)} %get-tuple-element.332, f32[16,512]{1,0:T(8,128)S(1)} %fusion.113, ...), kind=kOutput, calls=%fused_computation.5.clone.1 | convolution fusion | flops 1375731712 | bytes 39387140 | tf_op jit(solution)/shard_map/while/body/eval_jaxpr/hqk,khe->qhe/dot_general | solution.py:93
  193.6 4.6 constant_dynamic-slice_fusion.7
  198.3 14.3 %select_reduce_fusion.2 = (f32[16,512]{1,0:T(8,128)S(1)}, f32[16,512,1024]{2,1,0:T(8,128)}) fusion(pred[512,1024]{1,0:T(8,128)(4,1)S(1)} %fusion.112, bf16[1024,16,80]{0,2,1:T(8,128)(2,1)S(1)} %bitcast.193, bf16[2,512,16,80]{1,3,2,0:T(8,128)(2,1)S(1)} %get-tuple-element.373, s32[]{:T(128)S(6)} %copy.79), kind=kOutput, calls=%fused_computation.2.clone.1 | convolution fusion | flops 1358946304 | bytes 38043652 | tf_op jit(solution)/shard_map/while/body/eval_jaxpr/qhe,khe->hqk/dot_general | solution.py:29
  212.6 15.3 %fusion.113 = f32[16,512]{1,0:T(8,128)S(1)} fusion(f32[16,512,1024]{2,1,0:T(8,128)} %get-tuple-element.332, f32[16,512]{1,0:T(8,128)S(1)} %get-tuple-element.333, pred[512,1024]{1,0:T(8,128)(4,1)S(1)} %fusion.112), kind=kLoop, calls=%fused_computation.3.clone.1 | loop fusion | flops 25157632 | bytes 34144256 | tf_op jit(solution)/shard_map/while/body/eval_jaxpr/reduce_sum | solution.py:91
  228.0 14.3 %bitcast_dynamic-update-slice_fusion.6 = bf16[2,512,16,80]{1,3,2,0:T(8,128)(2,1)S(1)} fusion(bf16[2,512,16,80]{1,3,2,0:T(8,128)(2,1)S(1)} %copy-done.8, s32[]{:T(128)S(6)} %copy.79, bf16[1024,16,80]{0,2,1:T(8,128)(2,1)S(1)} %bitcast.196, f32[16,512,1024]{2,1,0:T(8,128)} %get-tuple-element.332, f32[16,512]{1,0:T(8,128)S(1)} %fusion.113, ...), kind=kOutput, calls=%fused_computation.5.clone.1 | convolution fusion | flops 1375731712 | bytes 39387140 | tf_op jit(solution)/shard_map/while/body/eval_jaxpr/hqk,khe->qhe/dot_general | solution.py:93
  250.6 9.7 multiply_reduce_fusion.3
  260.3 9.4 fusion.54
  269.7 10.1 convert_reduce_fusion.1
  279.8 4.5 multiply_reduce_fusion.1
  288.6 4.9 convolution_convert_fusion.4
  293.4 8.5 reshape.299
  302.0 7.2 copy.40
  311.0 272.4 %while.27 = (s32[]{:T(128)}, bf16[2,512,16,80]{1,3,2,0:T(8,128)(2,1)}, f32[2,1024,1280]{2,1,0:T(8,128)}, f32[2,1024,1280]{2,1,0:T(8,128)}, bf16[2,1024,1280]{1,2...) while((s32[]{:T(128)}, ...), condition=%wide.region_9.10_spmd, body=%wide.region_7.9_spmd.sunk | while | flops 6812591616 | bytes 374577376 | solution.py:170
  317.9 14.5 %fusion.123 = f32[16,512,1024]{2,1,0:T(8,128)} fusion(bf16[1024,16,80]{0,2,1:T(8,128)(2,1)S(1)} %bitcast.190, bf16[2,512,16,80]{1,3,2,0:T(8,128)(2,1)} %copy-done, s32[]{:T(128)S(6)} %copy.89), kind=kOutput, calls=%fused_computation.34.clone.1 | convolution fusion | flops 1342177280 | bytes 37486596 | tf_op jit(solution)/shard_map/while/body/eval_jaxpr/qhe,khe->hqk/dot_general | solution.py:29
  332.4 17.1 %fusion.125 = f32[16,80,1024]{2,1,0:T(8,128)} fusion(f32[16,512,1024]{2,1,0:T(8,128)} %fusion.123, f32[16,512]{1,0:T(8,128)S(1)} %dynamic-slice_bitcast_fusion.2, pred[512,1024]{1,0:T(8,128)(4,1)S(1)} %fusion.124, bf16[2,512,16,80]{1,3,2,0:T(8,128)(2,1)} %get-tuple-element.409, s32[]{:T(128)S(6)} %copy.89), kind=kOutput, calls=%fused_computation.22.clone.1 | convolution fusion | flops 1367343104 | bytes 40665092 | tf_op jit(solution)/shard_map/while/body/eval_jaxpr/hqk,qhe->khe/dot_general | solution.py:161
  349.5 5.9 copy.69
  355.4 25.5 %multiply_reduce_fusion.5 = (f32[16,512]{1,0:T(8,128)S(1)}, f32[16,512,1024]{2,1,0:T(8,128)}) fusion(f32[16,512,1024]{2,1,0:T(8,128)} %fusion.123, f32[16,512]{1,0:T(8,128)S(1)} %dynamic-slice_bitcast_fusion.2, pred[512,1024]{1,0:T(8,128)(4,1)S(1)} %fusion.124, bf16[1024,16,80]{0,2,1:T(8,128)(2,1)} %bitcast.195, ...), kind=kOutput, calls=%fused_computation.19.clone.1 | convolution fusion | flops 1375723520 | bytes 71630848 | tf_op jit(solution)/shard_map/while/body/eval_jaxpr/qhe,khe->hqk/dot_general | solution.py:150
  380.9 27.8 %multiply_convert_fusion.10 = bf16[16,512,1024]{2,1,0:T(8,128)(2,1)} fusion(f32[16,512,1024]{2,1,0:T(8,128)} %get-tuple-element.345, f32[16,512,1024]{2,1,0:T(8,128)} %fusion.123, f32[16,512]{1,0:T(8,128)S(1)} %get-tuple-element.346, f32[16,512]{1,0:T(8,128)S(1)} %dynamic-slice_bitcast_fusion.2, pred[512,1024]{1,0:T(8,128)(4,1)S(1)} %fusion.124), kind=kLoop, calls=%fused_computation.18.clone.1 | loop fusion | flops 41943040 | bytes 84475904 | tf_op jit(solution)/shard_map/while/body/eval_jaxpr/convert_element_type | solution.py:154
  408.7 12.1 %bitcast_dynamic-update-slice_fusion.8 = bf16[2,512,16,80]{1,3,2,0:T(8,128)(2,1)} fusion(bf16[2,512,16,80]{1,3,2,0:T(8,128)(2,1)} %get-tuple-element.389, s32[]{:T(128)S(6)} %copy.89, bf16[1024,16,80]{0,2,1:T(8,128)(2,1)S(1)} %bitcast.191, bf16[16,512,1024]{2,1,0:T(8,128)(2,1)} %multiply_convert_fusion.10), kind=kOutput, calls=%fused_computation.26.clone.1 | convolution fusion | flops 1342177280 | bytes 22020100 | tf_op jit(solution)/shard_map/while/body/eval_jaxpr/hqk,khe->qhe/dot_general | solution.py:155
  420.8 11.6 %fusion.126 = f32[16,80,1024]{2,1,0:T(8,128)} fusion(bf16[16,512,1024]{2,1,0:T(8,128)(2,1)} %multiply_convert_fusion.10, bf16[2,512,16,80]{1,3,2,0:T(8,128)(2,1)} %copy-done, s32[]{:T(128)S(6)} %copy.89), kind=kOutput, calls=%fused_computation.32.clone.1 | convolution fusion | flops 1342177280 | bytes 23330820 | tf_op jit(solution)/shard_map/while/body/eval_jaxpr/hqk,qhe->khe/dot_general | solution.py:158
  432.4 5.9 copy.70
  438.4 8.8 constant_dynamic-update-slice_fusion.3
  453.8 14.5 %fusion.123 = f32[16,512,1024]{2,1,0:T(8,128)} fusion(bf16[1024,16,80]{0,2,1:T(8,128)(2,1)S(1)} %bitcast.190, bf16[2,512,16,80]{1,3,2,0:T(8,128)(2,1)} %copy-done, s32[]{:T(128)S(6)} %copy.89), kind=kOutput, calls=%fused_computation.34.clone.1 | convolution fusion | flops 1342177280 | bytes 37486596 | tf_op jit(solution)/shard_map/while/body/eval_jaxpr/qhe,khe->hqk/dot_general | solution.py:29
  468.4 17.1 %fusion.125 = f32[16,80,1024]{2,1,0:T(8,128)} fusion(f32[16,512,1024]{2,1,0:T(8,128)} %fusion.123, f32[16,512]{1,0:T(8,128)S(1)} %dynamic-slice_bitcast_fusion.2, pred[512,1024]{1,0:T(8,128)(4,1)S(1)} %fusion.124, bf16[2,512,16,80]{1,3,2,0:T(8,128)(2,1)} %get-tuple-element.409, s32[]{:T(128)S(6)} %copy.89), kind=kOutput, calls=%fused_computation.22.clone.1 | convolution fusion | flops 1367343104 | bytes 40665092 | tf_op jit(solution)/shard_map/while/body/eval_jaxpr/hqk,qhe->khe/dot_general | solution.py:161
  485.5 5.9 copy.69
  491.3 25.5 %multiply_reduce_fusion.5 = (f32[16,512]{1,0:T(8,128)S(1)}, f32[16,512,1024]{2,1,0:T(8,128)}) fusion(f32[16,512,1024]{2,1,0:T(8,128)} %fusion.123, f32[16,512]{1,0:T(8,128)S(1)} %dynamic-slice_bitcast_fusion.2, pred[512,1024]{1,0:T(8,128)(4,1)S(1)} %fusion.124, bf16[1024,16,80]{0,2,1:T(8,128)(2,1)} %bitcast.195, ...), kind=kOutput, calls=%fused_computation.19.clone.1 | convolution fusion | flops 1375723520 | bytes 71630848 | tf_op jit(solution)/shard_map/while/body/eval_jaxpr/qhe,khe->hqk/dot_general | solution.py:150
  516.8 27.8 %multiply_convert_fusion.10 = bf16[16,512,1024]{2,1,0:T(8,128)(2,1)} fusion(f32[16,512,1024]{2,1,0:T(8,128)} %get-tuple-element.345, f32[16,512,1024]{2,1,0:T(8,128)} %fusion.123, f32[16,512]{1,0:T(8,128)S(1)} %get-tuple-element.346, f32[16,512]{1,0:T(8,128)S(1)} %dynamic-slice_bitcast_fusion.2, pred[512,1024]{1,0:T(8,128)(4,1)S(1)} %fusion.124), kind=kLoop, calls=%fused_computation.18.clone.1 | loop fusion | flops 41943040 | bytes 84475904 | tf_op jit(solution)/shard_map/while/body/eval_jaxpr/convert_element_type | solution.py:154
  544.7 12.0 %bitcast_dynamic-update-slice_fusion.8 = bf16[2,512,16,80]{1,3,2,0:T(8,128)(2,1)} fusion(bf16[2,512,16,80]{1,3,2,0:T(8,128)(2,1)} %get-tuple-element.389, s32[]{:T(128)S(6)} %copy.89, bf16[1024,16,80]{0,2,1:T(8,128)(2,1)S(1)} %bitcast.191, bf16[16,512,1024]{2,1,0:T(8,128)(2,1)} %multiply_convert_fusion.10), kind=kOutput, calls=%fused_computation.26.clone.1 | convolution fusion | flops 1342177280 | bytes 22020100 | tf_op jit(solution)/shard_map/while/body/eval_jaxpr/hqk,khe->qhe/dot_general | solution.py:155
  556.7 11.6 %fusion.126 = f32[16,80,1024]{2,1,0:T(8,128)} fusion(bf16[16,512,1024]{2,1,0:T(8,128)(2,1)} %multiply_convert_fusion.10, bf16[2,512,16,80]{1,3,2,0:T(8,128)(2,1)} %copy-done, s32[]{:T(128)S(6)} %copy.89), kind=kOutput, calls=%fused_computation.32.clone.1 | convolution fusion | flops 1342177280 | bytes 23330820 | tf_op jit(solution)/shard_map/while/body/eval_jaxpr/hqk,qhe->khe/dot_general | solution.py:158
  568.3 5.9 copy.70
  574.2 8.7 constant_dynamic-update-slice_fusion.3
  585.2 9.0 convolution_convert_fusion
  594.3 11.4 %convolution_convert_fusion.1 = bf16[1280,1280]{1,0:T(8,128)(2,1)} fusion(bf16[1024,1280]{1,0:T(8,128)(2,1)} %copy-done.47, f32[1024,1280]{1,0:T(8,128)} %get-tuple-element.212, f32[1280]{0:T(1024)S(1)} %copy-done.32, f32[1024]{0:T(1024)S(1)} %copy-done.30), kind=kOutput, calls=%fused_computation.57 | convolution fusion | flops 3361013760 | bytes 11150336 | tf_op jit(solution)/shard_map/nd,nf->df/dot_general | solution.py:130
  605.8 7.4 convolution_convert_fusion.2
  613.5 6.3 fusion.34
  624.9 5.1 convolution_convert_fusion.3
  634.3 5.1 fusion.32
  643.7 7.7 fusion.31
  652.2 8.7 fusion.55
  660.9 6.0 reduce-scatter.23.cloned.1.call-done
  667.0 41.2 %reduce-scatter.21.cloned.1.call-done = bf16[320,1280]{1,0:T(8,128)(2,1)} async-done(((bf16[1280,1280]{1,0:T(8,128)(2,1)}), bf16[320,1280]{1,0:T(8,128)(2,1)}) %reduce-scatter.21.cloned.1.call-update) | async-done | bytes 819216 | tf_op jit(solution)/shard_map/reduce_scatter | solution.py:213
  708.1 41.3 %reduce-scatter.19.cloned.1.call-done = bf16[320,1280]{1,0:T(8,128)(2,1)} async-done(((bf16[1280,1280]{1,0:T(8,128)(2,1)}), bf16[320,1280]{1,0:T(8,128)(2,1)}) %reduce-scatter.19.cloned.1.call-update) | async-done | bytes 819216 | tf_op jit(solution)/shard_map/reduce_scatter | solution.py:210
  749.4 41.2 %reduce-scatter.13.cloned.1.call-done = bf16[320,1280]{1,0:T(8,128)(2,1)} async-done(((bf16[1280,1280]{1,0:T(8,128)(2,1)}), bf16[320,1280]{1,0:T(8,128)(2,1)}) %reduce-scatter.13.cloned.1.call-update) | async-done | bytes 819216 | tf_op jit(solution)/shard_map/reduce_scatter | solution.py:201
  790.6 41.1 %reduce-scatter.17.cloned.1.call-done = bf16[320,1280]{1,0:T(8,128)(2,1)} async-done(((bf16[1280,1280]{1,0:T(8,128)(2,1)}), bf16[320,1280]{1,0:T(8,128)(2,1)}) %reduce-scatter.17.cloned.1.call-update) | async-done | bytes 819216 | tf_op jit(solution)/shard_map/reduce_scatter | solution.py:207
  831.7 41.2 %reduce-scatter.15.cloned.1.call-done = bf16[320,1280]{1,0:T(8,128)(2,1)} async-done(((bf16[1280,1280]{1,0:T(8,128)(2,1)}), bf16[320,1280]{1,0:T(8,128)(2,1)}) %reduce-scatter.15.cloned.1.call-update) | async-done | bytes 819216 | tf_op jit(solution)/shard_map/reduce_scatter | solution.py:204
  872.9 10.9 %add_convert_fusion = bf16[1024,1280]{1,0:T(8,128)(2,1)} fusion(f32[1024,1280]{1,0:T(8,128)} %get-tuple-element.212, bf16[1280,1280]{1,0:T(8,128)(2,1)} %all-gather.23.cloned.1.call-done, f32[1280]{0:T(1024)S(1)} %copy-done.40, f32[1024,1280]{1,0:T(8,128)} %fusion.54, f32[1280]{0:T(1024)S(1)} %copy-done.42), kind=kOutput, calls=%fused_computation.90 | convolution fusion | flops 3367239680 | bytes 16394240 | tf_op jit(solution)/shard_map/dot_general | solution.py:108
  888.9 6.3 fusion.46
  895.2 46.5 %all-reduce = (f32[1280]{0:T(1024)}, f32[1280]{0:T(1024)}, f32[1280]{0:T(1024)}, f32[1280]{0:T(1024)}, f32[80]{0:T(128)}) all-reduce(f32[1280]{0:T(1024)S(1)} %copy-done.33, f32[1280]{0:T(1024)S(1)} %convert_reduce_fusion, f32[1280]{0:T(1024)S(1)} %get-tuple-element.144, ...), channel_id=1, replica_groups=mesh['rep'=8,'fsdp'=2,'ctx'=2] {'rep','fsdp','ctx'}, use_global_device_ids=true, to_apply=%region_24.25 | all-reduce | flops 5200 | bytes 41600 | tf_op jit(solution)/shard_map/psum | solution.py:228
  941.7 6.0 fusion.43
  947.7 105.4 %all-reduce.4.cloned.1.call-done = (bf16[320,1280]{1,0:T(8,128)(2,1)}, bf16[320,1280]{1,0:T(8,128)(2,1)}, bf16[320,1280]{1,0:T(8,128)(2,1)}, bf16[320,1280]{1,0:...) async-done(((bf16[320,1280]{1,0:T(8,128)(2,1)}, bf16[320,1280]{1,0:T(8,128)(2,1)}, bf16[320,1280]{1,0:T(8,128)(2,1)}, bf16[320,1280]{1,0:T(8,128)(2,1)}, ...) | async-done | bytes 4915216 | tf_op jit(solution)/shard_map/psum | solution.py:221
  (203 shorter events, 80.0 us)
Async XLA Ops:
  7.2 5.2 copy-start.3
  7.2 34.4 %all-gather.15.cloned.1.call-start = ((), (), s32[]{:S(2)}) async-start(), calls=%async_computation.11 | async-start | bytes 4096000 | tf_op jit(solution)/shard_map/all_gather | solution.py:55
  7.9 64.5 %all-gather.9.cloned.1.call-start = ((), (), s32[]{:S(2)}) async-start(), calls=%async_computation.8 | async-start | bytes 4096000 | tf_op jit(solution)/shard_map/all_gather | solution.py:56
  8.7 94.6 %all-gather.13.cloned.1.call-start = ((), (), s32[]{:S(2)}) async-start(), calls=%async_computation.10 | async-start | bytes 4096000 | tf_op jit(solution)/shard_map/all_gather | solution.py:54
  9.4 110.5 %all-gather.17.cloned.1.call-start = ((), (), s32[]{:S(2)}) async-start(), calls=%async_computation.12 | async-start | bytes 7864320 | tf_op jit(solution)/shard_map/all_gather | solution.py:80
  53.9 84.4 %all-gather.11.cloned.1.call-start = ((), (), s32[]{:S(2)}) async-start(), calls=%async_computation.9 | async-start | bytes 7864320 | tf_op jit(solution)/shard_map/all_gather | solution.py:81
  80.2 6.9 copy-start.44
  80.2 6.9 copy-start.25
  84.7 165.9 %all-gather.19.cloned.1.call-start = ((), (), s32[]{:S(2)}) async-start(), calls=%async_computation.13 | async-start | bytes 4096000 | tf_op jit(solution)/shard_map/all_gather | solution.py:57
  85.3 175.0 %all-gather.21.cloned.1.call-start = ((), (), s32[]{:S(2)}) async-start(), calls=%async_computation.14 | async-start | bytes 4096000 | tf_op jit(solution)/shard_map/all_gather | solution.py:58
  86.1 183.7 %all-gather.23.cloned.1.call-start = ((), (), s32[]{:S(2)}) async-start(), calls=%async_computation.15 | async-start | bytes 4096000 | tf_op jit(solution)/shard_map/all_gather | solution.py:59
  86.8 543.3 %reduce-scatter.11.cloned.1.call-start = ((), (), s32[]{:S(2)}) async-start(), calls=%async_computation.17 | async-start | bytes 15728640 | tf_op jit(solution)/shard_map/reduce_scatter | solution.py:175
  87.1 21.8 %copy-start.35 = (f32[80]{0:T(128)}, f32[80]{0:T(128)S(1)}, u32[]{:S(2)}) copy-start(f32[80]{0:T(128)S(1)} %fusion.51) | copy-start | bytes 964
  108.9 31.2 %copy-start.43 = (s32[2]{0:T(128)S(1)}, s32[2]{0:T(128)}, u32[]{:S(2)}) copy-start(s32[2]{0:T(128)} %param.19) | copy-start | bytes 28
  159.9 15.4 %copy-start.5 = (bf16[1,1024,1280]{1,2,0:T(8,128)(2,1)S(1)}, bf16[1,1024,1280]{1,2,0:T(8,128)(2,1)}, u32[]{:S(2)}) copy-start(bf16[1,1024,1280]{1,2,0:T(8,128)(2,1)} %get-tuple-element.330) | copy-start | bytes 7864324 | tf_op jit(solution)/shard_map/while
  159.9 15.4 %copy-start.8 = (bf16[2,512,16,80]{1,3,2,0:T(8,128)(2,1)S(1)}, bf16[2,512,16,80]{1,3,2,0:T(8,128)(2,1)}, u32[]{:S(2)}) copy-start(bf16[2,512,16,80]{1,3,2,0:T(8,128)(2,1)} %get-tuple-element.359) | copy-start | bytes 7864324 | tf_op jit(solution)/shard_map/while
  212.6 15.4 %copy-start.5 = (bf16[1,1024,1280]{1,2,0:T(8,128)(2,1)S(1)}, bf16[1,1024,1280]{1,2,0:T(8,128)(2,1)}, u32[]{:S(2)}) copy-start(bf16[1,1024,1280]{1,2,0:T(8,128)(2,1)} %get-tuple-element.330) | copy-start | bytes 7864324 | tf_op jit(solution)/shard_map/while
  212.6 15.4 %copy-start.8 = (bf16[2,512,16,80]{1,3,2,0:T(8,128)(2,1)S(1)}, bf16[2,512,16,80]{1,3,2,0:T(8,128)(2,1)}, u32[]{:S(2)}) copy-start(bf16[2,512,16,80]{1,3,2,0:T(8,128)(2,1)} %get-tuple-element.359) | copy-start | bytes 7864324 | tf_op jit(solution)/shard_map/while
  250.6 9.7 copy-start.31
  260.3 24.0 %copy-start.29 = (f32[1024]{0:T(1024)}, f32[1024]{0:T(1024)S(1)}, u32[]{:S(2)}) copy-start(f32[1024]{0:T(1024)S(1)} %get-tuple-element.206) | copy-start | bytes 12292
  260.3 9.4 copy-start.41
  269.7 10.1 copy-start.7
  269.7 10.1 copy-start.39
  279.8 4.5 copy-start.47
  279.8 4.5 copy-start.11
  284.3 4.3 copy-start.14
  286.2 2.4 copy-start.6
  311.2 6.5 copy-start
  311.2 6.4 copy-start.2
  438.3 8.8 copy-start.1
  447.2 6.4 copy-start
  447.2 6.4 copy-start.2
  574.2 8.8 copy-start.1
  583.4 56.1 %reduce-scatter.9.cloned.1.call-start = ((), (), s32[]{:S(2)}) async-start(), calls=%async_computation.16 | async-start | bytes 15728640 | tf_op jit(solution)/shard_map/reduce_scatter | solution.py:174
  583.5 1.7 copy-start.12
  583.5 1.7 copy-start.42
  584.0 10.3 copy-start.30
  584.0 10.3 copy-start.32
  584.0 82.9 %reduce-scatter.23.cloned.1.call-start = ((), (), s32[]{:S(2)}) async-start(), calls=%async_computation.23 | async-start | bytes 4096000 | tf_op jit(solution)/shard_map/reduce_scatter | solution.py:216
  594.2 11.6 %copy-start.10 = (bf16[160,8,2,512]{3,1,2,0:T(8,128)(2,1)S(1)}, bf16[160,8,2,512]{3,1,2,0:T(8,128)(2,1)}, u32[]{:S(2)}) copy-start(bf16[160,8,2,512]{3,1,2,0:T(8,128)(2,1)} %copy.65) | copy-start | bytes 7864324
  594.3 113.9 %reduce-scatter.21.cloned.1.call-start = ((), (), s32[]{:S(2)}) async-start(), calls=%async_computation.22 | async-start | bytes 4096000 | tf_op jit(solution)/shard_map/reduce_scatter | solution.py:213
  605.8 7.8 copy-start.36
  605.8 143.6 %reduce-scatter.19.cloned.1.call-start = ((), (), s32[]{:S(2)}) async-start(), calls=%async_computation.21 | async-start | bytes 4096000 | tf_op jit(solution)/shard_map/reduce_scatter | solution.py:210
  613.3 177.3 %reduce-scatter.13.cloned.1.call-start = ((), (), s32[]{:S(2)}) async-start(), calls=%async_computation.18 | async-start | bytes 4096000 | tf_op jit(solution)/shard_map/reduce_scatter | solution.py:201
  619.9 5.0 copy-start.16
  630.0 201.7 %reduce-scatter.17.cloned.1.call-start = ((), (), s32[]{:S(2)}) async-start(), calls=%async_computation.20 | async-start | bytes 4096000 | tf_op jit(solution)/shard_map/reduce_scatter | solution.py:207
  639.4 233.5 %reduce-scatter.15.cloned.1.call-start = ((), (), s32[]{:S(2)}) async-start(), calls=%async_computation.19 | async-start | bytes 4096000 | tf_op jit(solution)/shard_map/reduce_scatter | solution.py:204
  643.7 8.0 copy-start.28
  643.7 8.0 copy-start.13
  651.4 401.7 %all-reduce.4.cloned.1.call-start = ((), (), s32[]{:S(2)}) async-start(), calls=%async_computation.24 | async-start | bytes 9830400 | tf_op jit(solution)/shard_map/psum | solution.py:221
  652.2 220.7 %copy-start.40 = (f32[1280]{0:T(1024)S(1)}, f32[1280]{0:T(1024)}, u32[]{:S(2)}) copy-start(f32[1280]{0:T(1024)} %param.27) | copy-start | bytes 15364
  872.9 10.9 %copy-start.20 = (bf16[2,512,1280]{2,1,0:T(8,128)(2,1)S(1)}, bf16[2,512,1280]{2,1,0:T(8,128)(2,1)}, u32[]{:S(2)}) copy-start(bf16[2,512,1280]{2,1,0:T(8,128)(2,1)} %copy-done.19) | copy-start | bytes 7864324
  872.9 10.9 %copy-start.37 = (bf16[1280,1280]{1,0:T(8,128)(2,1)S(1)}, bf16[1280,1280]{1,0:T(8,128)(2,1)}, u32[]{:S(2)}) copy-start(bf16[1280,1280]{1,0:T(8,128)(2,1)} %all-gather.15.cloned.1.call-done) | copy-start | bytes 9830404
  883.8 3.6 copy-start.4
  883.8 3.6 copy-start.18
  883.8 3.6 copy-start.26
  883.9 3.6 copy-start.38
  883.9 5.0 copy-start.46
  888.9 6.3 copy-start.33
  888.9 6.3 copy-start.34
  1053.1 5.1 copy-start.24
  1053.1 6.3 copy-start.23
  1053.1 7.6 copy-start.22
  1055.7 6.3 copy-start.21
  (7 other events, 8.9 us)
Sparse Core Ops, SparseCore 0:
  9.6 31.9 all-gather.14
  43.1 29.2 all-gather.8
  74.0 29.2 all-gather.12
  104.7 15.2 all-gather.16
  121.9 16.3 all-gather.10
  139.7 30.4 all-gather.18
  171.7 29.2 all-gather.20
  202.6 29.2 all-gather.22
  583.5 19.3 reduce-scatter.10
  605.0 19.2 reduce-scatter.8
  626.9 39.9 reduce-scatter.22
  669.4 38.6 reduce-scatter.20
  710.7 38.6 reduce-scatter.18
  751.8 38.6 reduce-scatter.12
  793.0 38.6 reduce-scatter.16
  834.1 38.6 reduce-scatter.14
  877.1 175.9 all-reduce.3
where the time goes:
time: 1080 us; the launch traced here: 1070 us
  waiting for transfers between devices  401 us (37%)
  matrix products  357 us (33%)
  other arithmetic  131 us (12%)
  local copies, waits for them, and re-layouts  118 us (11%)
  blocking collectives  46.5 us (4%)
  between operations  14.7 us (1%)
    psum x1, waiting for transfers between devices, shards(): lax.psum(query_shard.astype(jnp.bfloat16), 'rep').astype(jnp.float32)  105 us
    dot_general x4, matrix products, masked_scores(): jnp.einsum('qhe,khe->hqk', queries, keys, preferred_element_type=jnp.floa...  57 us
    convert_element_type x2, other arithmetic, backward_one(): score_grad = (exact_prob * (prob_grad - row_inner)).astype(jnp.bfloat16)  55.7 us
    dot_general x2, matrix products, backward_one(): jnp.einsum('qhe,khe->hqk', grad_seq, values_heads, preferred_element_type...  51 us
    psum x1, blocking collectives, shards(): lax.psum((upbias_part, downbias_part, attngain_part, mlpgain_part, scale_...  46.5 us
    reduce_scatter x1, waiting for transfers between devices, shards(): lax.psum_scatter(output_part.astype(jnp.bfloat16), ('fsdp', 'ctx'), scatt...  41.3 us
    dynamic_update_slice x6, local copies, waits for them, and re-layouts, shards(): lax.map(backward_one, (queries, key_back, value_back, context_grad, logsu...  41.2 us
    reduce_scatter x1, waiting for transfers between devices, shards(): lax.psum_scatter(up_part.astype(jnp.bfloat16), ('fsdp', 'ctx'), scatter_d...  41.2 us
  transfers between devices with their start and end apart: 17, of which 12 were waited for; matrix products, arithmetic and copies ran while one was open for 25% of the time, Pallas kernels for 0%

commit v1 on v0

--- a/solution.py
+++ b/solution.py
@@ -218,7 +218,9 @@
         ).astype(jnp.float32),
     )
     query_total, key_total, value_total, output_total, up_total, down_total = (
-        lax.psum(query_shard.astype(jnp.bfloat16), "rep").astype(jnp.float32),
+        jnp.sum(lax.all_gather(query_shard.astype(jnp.bfloat16), "rep"), axis=0).astype(
+            jnp.float32
+        ),
         lax.psum(key_shard.astype(jnp.bfloat16), "rep").astype(jnp.float32),
         lax.psum(value_shard.astype(jnp.bfloat16), "rep").astype(jnp.float32),
         lax.psum(output_shard.astype(jnp.bfloat16), "rep").astype(jnp.float32),

time: 1080 us -> 1160 us (1.074)
  waiting for transfers between devices: 401 us -> 483 us
    all_gather x0 -> x1, waiting for transfers between devices: none -> 96.3 us  [shards(): lax.all_gather(query_shard.astype(jnp.bfloat16), 'rep')]
    reduce_scatter x1, waiting for transfers between devices: 6.04 us -> 29.5 us  [shards(): lax.psum_scatter(down_part.astype(jnp.bfloat16), ('fsdp', 'ctx'), scatter...]
    reduce_scatter x1, waiting for transfers between devices: 41.2 us -> 19.7 us  [shards(): lax.psum_scatter(query_part.astype(jnp.bfloat16), ('fsdp', 'ctx'), scatte...]
    psum x1, waiting for transfers between devices: 105 us -> 88.8 us  [shards(): lax.psum(key_shard.astype(jnp.bfloat16), 'rep').astype(jnp.float32)]
  transfers between devices with their start and end apart: 17 -> 18, of which waited for: 12 -> 13; matrix products, arithmetic and copies ran while one was open for 25% -> 24% of each run, Pallas kernels for 0% -> 0%
where the time goes in v1:
time: 1160 us; the launch traced here: 1150 us
  waiting for transfers between devices  483 us (42%)
  matrix products  359 us (31%)
  other arithmetic  132 us (11%)
  local copies, waits for them, and re-layouts  116 us (10%)
  blocking collectives  42.7 us (4%)
  between operations  15.1 us (1%)
    all_gather x1, waiting for transfers between devices, shards(): lax.all_gather(query_shard.astype(jnp.bfloat16), 'rep')  96.3 us
    psum x1, waiting for transfers between devices, shards(): lax.psum(key_shard.astype(jnp.bfloat16), 'rep').astype(jnp.float32)  88.8 us
    dot_general x4, matrix products, masked_scores(): jnp.einsum('qhe,khe->hqk', queries, keys, preferred_element_type=jnp.floa...  56.9 us
    convert_element_type x2, other arithmetic, backward_one(): score_grad = (exact_prob * (prob_grad - row_inner)).astype(jnp.bfloat16)  55.7 us
    dot_general x2, matrix products, backward_one(): jnp.einsum('qhe,khe->hqk', grad_seq, values_heads, preferred_element_type...  50.9 us
    psum x1, blocking collectives, shards(): lax.psum((upbias_part, downbias_part, attngain_part, mlpgain_part, scale_...  42.7 us
    reduce_scatter x1, waiting for transfers between devices, shards(): lax.psum_scatter(up_part.astype(jnp.bfloat16), ('fsdp', 'ctx'), scatter_d...  41.3 us
    dynamic_update_slice x6, local copies, waits for them, and re-layouts, shards(): lax.map(backward_one, (queries, key_back, value_back, context_grad, logsu...  41.3 us
  transfers between devices with their start and end apart: 18, of which 13 were waited for; matrix products, arithmetic and copies ran while one was open for 24% of the time, Pallas kernels for 0%

profile of v1, /device:TPU:0, one launch (start us, length us, event | category | flops | bytes accessed | tf_op | source)
XLA Modules:
  0.0 1150.2 jit_solution(16950238218163220654)
XLA Ops:
  15.3 26.3 %all-gather.17.cloned.1.call-done = bf16[1280,1280]{1,0:T(8,128)(2,1)} async-done(((bf16[320,1280]{1,0:T(8,128)(2,1)}), bf16[1280,1280]{1,0:T(8,128)(2,1)}) %all-gather.17.cloned.1.call-update) | async-done | bytes 3276816 | tf_op jit(solution)/shard_map/all_gather | solution.py:55
  41.6 7.8 convolution_convert_fusion.5
  49.3 4.5 copy.37
  53.9 18.5 %all-gather.11.cloned.1.call-done = bf16[1280,1280]{1,0:T(8,128)(2,1)} async-done(((bf16[320,1280]{1,0:T(8,128)(2,1)}), bf16[1280,1280]{1,0:T(8,128)(2,1)}) %all-gather.11.cloned.1.call-update) | async-done | bytes 3276816 | tf_op jit(solution)/shard_map/all_gather | solution.py:56
  72.4 7.8 convolution_convert_fusion.6
  80.2 4.5 copy.35
  89.3 14.0 %all-gather.15.cloned.1.call-done = bf16[1280,1280]{1,0:T(8,128)(2,1)} async-done(((bf16[320,1280]{1,0:T(8,128)(2,1)}), bf16[1280,1280]{1,0:T(8,128)(2,1)}) %all-gather.15.cloned.1.call-update) | async-done | bytes 3276816 | tf_op jit(solution)/shard_map/all_gather | solution.py:54
  103.3 5.6 copy.36
  108.9 9.2 multiply_convert_fusion.4
  119.9 18.4 %all-gather.13.cloned.1.call-done = bf16[2,1024,1280]{1,2,0:T(8,128)(2,1)} async-done(((bf16[2,512,1280]{1,2,0:T(8,128)(2,1)}), bf16[2,1024,1280]{1,2,0:T(8,128)(2,1)}) %all-gather.13.cloned.1.call-update) | async-done | bytes 5242896 | tf_op jit(solution)/shard_map/all_gather | solution.py:81
  140.1 103.9 %while.26 = (s32[]{:T(128)}, bf16[2,512,16,80]{1,3,2,0:T(8,128)(2,1)}, f32[2,16,512,1]{2,1,3,0:T(8,128)S(1)}, bf16[2,1024,1280]{1,2,0:T(8,128)(2,1)}, s32[]{:T(1...) while((s32[]{:T(128)}, ...), condition=%wide.region_4.5_spmd, body=%wide.region_1.4_spmd.sunk | while | flops 2760893952 | bytes 154147024 | solution.py:101
  141.7 4.6 constant_dynamic-slice_fusion.7
  146.4 13.5 %select_reduce_fusion.2 = (f32[16,512]{1,0:T(8,128)S(1)}, f32[16,512,1024]{2,1,0:T(8,128)}) fusion(pred[512,1024]{1,0:T(8,128)(4,1)S(1)} %fusion.112, bf16[1024,16,80]{0,2,1:T(8,128)(2,1)S(1)} %bitcast.194, bf16[2,512,16,80]{1,3,2,0:T(8,128)(2,1)S(1)} %get-tuple-element.372, s32[]{:T(128)S(6)} %copy.79), kind=kOutput, calls=%fused_computation.2.clone.1 | convolution fusion | flops 1358946304 | bytes 38043652 | tf_op jit(solution)/shard_map/while/body/eval_jaxpr/qhe,khe->hqk/dot_general | solution.py:29
  159.9 15.4 %fusion.113 = f32[16,512]{1,0:T(8,128)S(1)} fusion(f32[16,512,1024]{2,1,0:T(8,128)} %get-tuple-element.331, f32[16,512]{1,0:T(8,128)S(1)} %get-tuple-element.332, pred[512,1024]{1,0:T(8,128)(4,1)S(1)} %fusion.112), kind=kLoop, calls=%fused_computation.3.clone.1 | loop fusion | flops 25157632 | bytes 34144256 | tf_op jit(solution)/shard_map/while/body/eval_jaxpr/reduce_sum | solution.py:91
  175.3 15.2 %bitcast_dynamic-update-slice_fusion.6 = bf16[2,512,16,80]{1,3,2,0:T(8,128)(2,1)S(1)} fusion(bf16[2,512,16,80]{1,3,2,0:T(8,128)(2,1)S(1)} %copy-done.8, s32[]{:T(128)S(6)} %copy.79, bf16[1024,16,80]{0,2,1:T(8,128)(2,1)S(1)} %bitcast.197, f32[16,512,1024]{2,1,0:T(8,128)} %get-tuple-element.331, f32[16,512]{1,0:T(8,128)S(1)} %fusion.113, ...), kind=kOutput, calls=%fused_computation.5.clone.1 | convolution fusion | flops 1375731712 | bytes 39387140 | tf_op jit(solution)/shard_map/while/body/eval_jaxpr/hqk,khe->qhe/dot_general | solution.py:93
  193.7 4.6 constant_dynamic-slice_fusion.7
  198.3 14.3 %select_reduce_fusion.2 = (f32[16,512]{1,0:T(8,128)S(1)}, f32[16,512,1024]{2,1,0:T(8,128)}) fusion(pred[512,1024]{1,0:T(8,128)(4,1)S(1)} %fusion.112, bf16[1024,16,80]{0,2,1:T(8,128)(2,1)S(1)} %bitcast.194, bf16[2,512,16,80]{1,3,2,0:T(8,128)(2,1)S(1)} %get-tuple-element.372, s32[]{:T(128)S(6)} %copy.79), kind=kOutput, calls=%fused_computation.2.clone.1 | convolution fusion | flops 1358946304 | bytes 38043652 | tf_op jit(solution)/shard_map/while/body/eval_jaxpr/qhe,khe->hqk/dot_general | solution.py:29
  212.6 15.3 %fusion.113 = f32[16,512]{1,0:T(8,128)S(1)} fusion(f32[16,512,1024]{2,1,0:T(8,128)} %get-tuple-element.331, f32[16,512]{1,0:T(8,128)S(1)} %get-tuple-element.332, pred[512,1024]{1,0:T(8,128)(4,1)S(1)} %fusion.112), kind=kLoop, calls=%fused_computation.3.clone.1 | loop fusion | flops 25157632 | bytes 34144256 | tf_op jit(solution)/shard_map/while/body/eval_jaxpr/reduce_sum | solution.py:91
  228.0 14.3 %bitcast_dynamic-update-slice_fusion.6 = bf16[2,512,16,80]{1,3,2,0:T(8,128)(2,1)S(1)} fusion(bf16[2,512,16,80]{1,3,2,0:T(8,128)(2,1)S(1)} %copy-done.8, s32[]{:T(128)S(6)} %copy.79, bf16[1024,16,80]{0,2,1:T(8,128)(2,1)S(1)} %bitcast.197, f32[16,512,1024]{2,1,0:T(8,128)} %get-tuple-element.331, f32[16,512]{1,0:T(8,128)S(1)} %fusion.113, ...), kind=kOutput, calls=%fused_computation.5.clone.1 | convolution fusion | flops 1375731712 | bytes 39387140 | tf_op jit(solution)/shard_map/while/body/eval_jaxpr/hqk,khe->qhe/dot_general | solution.py:93
  250.6 9.7 multiply_reduce_fusion.3
  260.4 9.4 fusion.54
  269.8 10.1 convert_reduce_fusion.1
  288.6 4.9 convolution_convert_fusion.4
  293.5 8.5 reshape.300
  302.0 7.2 copy.40
  311.1 272.3 %while.27 = (s32[]{:T(128)}, bf16[2,512,16,80]{1,3,2,0:T(8,128)(2,1)}, f32[2,1024,1280]{2,1,0:T(8,128)}, f32[2,1024,1280]{2,1,0:T(8,128)}, bf16[2,1024,1280]{1,2...) while((s32[]{:T(128)}, ...), condition=%wide.region_9.10_spmd, body=%wide.region_7.9_spmd.sunk | while | flops 6812591616 | bytes 374577376 | solution.py:170
  317.9 14.5 %fusion.123 = f32[16,512,1024]{2,1,0:T(8,128)} fusion(bf16[1024,16,80]{0,2,1:T(8,128)(2,1)S(1)} %bitcast.191, bf16[2,512,16,80]{1,3,2,0:T(8,128)(2,1)} %copy-done, s32[]{:T(128)S(6)} %copy.89), kind=kOutput, calls=%fused_computation.34.clone.1 | convolution fusion | flops 1342177280 | bytes 37486596 | tf_op jit(solution)/shard_map/while/body/eval_jaxpr/qhe,khe->hqk/dot_general | solution.py:29
  332.4 17.1 %fusion.125 = f32[16,80,1024]{2,1,0:T(8,128)} fusion(f32[16,512,1024]{2,1,0:T(8,128)} %fusion.123, f32[16,512]{1,0:T(8,128)S(1)} %dynamic-slice_bitcast_fusion.2, pred[512,1024]{1,0:T(8,128)(4,1)S(1)} %fusion.124, bf16[2,512,16,80]{1,3,2,0:T(8,128)(2,1)} %get-tuple-element.408, s32[]{:T(128)S(6)} %copy.89), kind=kOutput, calls=%fused_computation.22.clone.1 | convolution fusion | flops 1367343104 | bytes 40665092 | tf_op jit(solution)/shard_map/while/body/eval_jaxpr/hqk,qhe->khe/dot_general | solution.py:161
  349.5 5.9 copy.69
  355.4 25.4 %multiply_reduce_fusion.5 = (f32[16,512]{1,0:T(8,128)S(1)}, f32[16,512,1024]{2,1,0:T(8,128)}) fusion(f32[16,512,1024]{2,1,0:T(8,128)} %fusion.123, f32[16,512]{1,0:T(8,128)S(1)} %dynamic-slice_bitcast_fusion.2, pred[512,1024]{1,0:T(8,128)(4,1)S(1)} %fusion.124, bf16[1024,16,80]{0,2,1:T(8,128)(2,1)} %bitcast.196, ...), kind=kOutput, calls=%fused_computation.19.clone.1 | convolution fusion | flops 1375723520 | bytes 71630848 | tf_op jit(solution)/shard_map/while/body/eval_jaxpr/qhe,khe->hqk/dot_general | solution.py:150
  380.8 27.8 %multiply_convert_fusion.10 = bf16[16,512,1024]{2,1,0:T(8,128)(2,1)} fusion(f32[16,512,1024]{2,1,0:T(8,128)} %get-tuple-element.344, f32[16,512,1024]{2,1,0:T(8,128)} %fusion.123, f32[16,512]{1,0:T(8,128)S(1)} %get-tuple-element.345, f32[16,512]{1,0:T(8,128)S(1)} %dynamic-slice_bitcast_fusion.2, pred[512,1024]{1,0:T(8,128)(4,1)S(1)} %fusion.124), kind=kLoop, calls=%fused_computation.18.clone.1 | loop fusion | flops 41943040 | bytes 84475904 | tf_op jit(solution)/shard_map/while/body/eval_jaxpr/convert_element_type | solution.py:154
  408.7 12.1 %bitcast_dynamic-update-slice_fusion.8 = bf16[2,512,16,80]{1,3,2,0:T(8,128)(2,1)} fusion(bf16[2,512,16,80]{1,3,2,0:T(8,128)(2,1)} %get-tuple-element.388, s32[]{:T(128)S(6)} %copy.89, bf16[1024,16,80]{0,2,1:T(8,128)(2,1)S(1)} %bitcast.192, bf16[16,512,1024]{2,1,0:T(8,128)(2,1)} %multiply_convert_fusion.10), kind=kOutput, calls=%fused_computation.26.clone.1 | convolution fusion | flops 1342177280 | bytes 22020100 | tf_op jit(solution)/shard_map/while/body/eval_jaxpr/hqk,khe->qhe/dot_general | solution.py:155
  420.8 11.6 %fusion.126 = f32[16,80,1024]{2,1,0:T(8,128)} fusion(bf16[16,512,1024]{2,1,0:T(8,128)(2,1)} %multiply_convert_fusion.10, bf16[2,512,16,80]{1,3,2,0:T(8,128)(2,1)} %copy-done, s32[]{:T(128)S(6)} %copy.89), kind=kOutput, calls=%fused_computation.32.clone.1 | convolution fusion | flops 1342177280 | bytes 23330820 | tf_op jit(solution)/shard_map/while/body/eval_jaxpr/hqk,qhe->khe/dot_general | solution.py:158
  432.4 5.9 copy.70
  438.3 8.8 constant_dynamic-update-slice_fusion.3
  453.8 14.5 %fusion.123 = f32[16,512,1024]{2,1,0:T(8,128)} fusion(bf16[1024,16,80]{0,2,1:T(8,128)(2,1)S(1)} %bitcast.191, bf16[2,512,16,80]{1,3,2,0:T(8,128)(2,1)} %copy-done, s32[]{:T(128)S(6)} %copy.89), kind=kOutput, calls=%fused_computation.34.clone.1 | convolution fusion | flops 1342177280 | bytes 37486596 | tf_op jit(solution)/shard_map/while/body/eval_jaxpr/qhe,khe->hqk/dot_general | solution.py:29
  468.3 17.1 %fusion.125 = f32[16,80,1024]{2,1,0:T(8,128)} fusion(f32[16,512,1024]{2,1,0:T(8,128)} %fusion.123, f32[16,512]{1,0:T(8,128)S(1)} %dynamic-slice_bitcast_fusion.2, pred[512,1024]{1,0:T(8,128)(4,1)S(1)} %fusion.124, bf16[2,512,16,80]{1,3,2,0:T(8,128)(2,1)} %get-tuple-element.408, s32[]{:T(128)S(6)} %copy.89), kind=kOutput, calls=%fused_computation.22.clone.1 | convolution fusion | flops 1367343104 | bytes 40665092 | tf_op jit(solution)/shard_map/while/body/eval_jaxpr/hqk,qhe->khe/dot_general | solution.py:161
  485.4 5.9 copy.69
  491.3 25.4 %multiply_reduce_fusion.5 = (f32[16,512]{1,0:T(8,128)S(1)}, f32[16,512,1024]{2,1,0:T(8,128)}) fusion(f32[16,512,1024]{2,1,0:T(8,128)} %fusion.123, f32[16,512]{1,0:T(8,128)S(1)} %dynamic-slice_bitcast_fusion.2, pred[512,1024]{1,0:T(8,128)(4,1)S(1)} %fusion.124, bf16[1024,16,80]{0,2,1:T(8,128)(2,1)} %bitcast.196, ...), kind=kOutput, calls=%fused_computation.19.clone.1 | convolution fusion | flops 1375723520 | bytes 71630848 | tf_op jit(solution)/shard_map/while/body/eval_jaxpr/qhe,khe->hqk/dot_general | solution.py:150
  516.7 27.8 %multiply_convert_fusion.10 = bf16[16,512,1024]{2,1,0:T(8,128)(2,1)} fusion(f32[16,512,1024]{2,1,0:T(8,128)} %get-tuple-element.344, f32[16,512,1024]{2,1,0:T(8,128)} %fusion.123, f32[16,512]{1,0:T(8,128)S(1)} %get-tuple-element.345, f32[16,512]{1,0:T(8,128)S(1)} %dynamic-slice_bitcast_fusion.2, pred[512,1024]{1,0:T(8,128)(4,1)S(1)} %fusion.124), kind=kLoop, calls=%fused_computation.18.clone.1 | loop fusion | flops 41943040 | bytes 84475904 | tf_op jit(solution)/shard_map/while/body/eval_jaxpr/convert_element_type | solution.py:154
  544.6 12.0 %bitcast_dynamic-update-slice_fusion.8 = bf16[2,512,16,80]{1,3,2,0:T(8,128)(2,1)} fusion(bf16[2,512,16,80]{1,3,2,0:T(8,128)(2,1)} %get-tuple-element.388, s32[]{:T(128)S(6)} %copy.89, bf16[1024,16,80]{0,2,1:T(8,128)(2,1)S(1)} %bitcast.192, bf16[16,512,1024]{2,1,0:T(8,128)(2,1)} %multiply_convert_fusion.10), kind=kOutput, calls=%fused_computation.26.clone.1 | convolution fusion | flops 1342177280 | bytes 22020100 | tf_op jit(solution)/shard_map/while/body/eval_jaxpr/hqk,khe->qhe/dot_general | solution.py:155
  556.6 11.6 %fusion.126 = f32[16,80,1024]{2,1,0:T(8,128)} fusion(bf16[16,512,1024]{2,1,0:T(8,128)(2,1)} %multiply_convert_fusion.10, bf16[2,512,16,80]{1,3,2,0:T(8,128)(2,1)} %copy-done, s32[]{:T(128)S(6)} %copy.89), kind=kOutput, calls=%fused_computation.32.clone.1 | convolution fusion | flops 1342177280 | bytes 23330820 | tf_op jit(solution)/shard_map/while/body/eval_jaxpr/hqk,qhe->khe/dot_general | solution.py:158
  568.2 5.9 copy.70
  574.1 8.8 constant_dynamic-update-slice_fusion.3
  593.8 5.1 convolution_convert_fusion.3
  599.0 10.0 convolution_convert_fusion
  609.3 9.9 convolution_convert_fusion.1
  619.3 8.8 convolution_convert_fusion.2
  632.5 5.1 fusion.32
  642.0 5.1 fusion.31
  647.2 19.7 %reduce-scatter.13.cloned.1.call-done = bf16[320,1280]{1,0:T(8,128)(2,1)} async-done(((bf16[1280,1280]{1,0:T(8,128)(2,1)}), bf16[320,1280]{1,0:T(8,128)(2,1)}) %reduce-scatter.13.cloned.1.call-update) | async-done | bytes 819216 | tf_op jit(solution)/shard_map/reduce_scatter | solution.py:201
  667.7 10.9 add_convert_fusion
  678.6 29.5 %reduce-scatter.23.cloned.1.call-done = bf16[320,1280]{1,0:T(8,128)(2,1)} async-done(((bf16[1280,1280]{1,0:T(8,128)(2,1)}), bf16[320,1280]{1,0:T(8,128)(2,1)}) %reduce-scatter.23.cloned.1.call-update) | async-done | bytes 819216 | tf_op jit(solution)/shard_map/reduce_scatter | solution.py:216
  708.1 41.3 %reduce-scatter.21.cloned.1.call-done = bf16[320,1280]{1,0:T(8,128)(2,1)} async-done(((bf16[1280,1280]{1,0:T(8,128)(2,1)}), bf16[320,1280]{1,0:T(8,128)(2,1)}) %reduce-scatter.21.cloned.1.call-update) | async-done | bytes 819216 | tf_op jit(solution)/shard_map/reduce_scatter | solution.py:213
  749.4 41.2 %reduce-scatter.19.cloned.1.call-done = bf16[320,1280]{1,0:T(8,128)(2,1)} async-done(((bf16[1280,1280]{1,0:T(8,128)(2,1)}), bf16[320,1280]{1,0:T(8,128)(2,1)}) %reduce-scatter.19.cloned.1.call-update) | async-done | bytes 819216 | tf_op jit(solution)/shard_map/reduce_scatter | solution.py:210
  790.6 41.2 %reduce-scatter.17.cloned.1.call-done = bf16[320,1280]{1,0:T(8,128)(2,1)} async-done(((bf16[1280,1280]{1,0:T(8,128)(2,1)}), bf16[320,1280]{1,0:T(8,128)(2,1)}) %reduce-scatter.17.cloned.1.call-update) | async-done | bytes 819216 | tf_op jit(solution)/shard_map/reduce_scatter | solution.py:207
  831.7 41.2 %reduce-scatter.15.cloned.1.call-done = bf16[320,1280]{1,0:T(8,128)(2,1)} async-done(((bf16[1280,1280]{1,0:T(8,128)(2,1)}), bf16[320,1280]{1,0:T(8,128)(2,1)}) %reduce-scatter.15.cloned.1.call-update) | async-done | bytes 819216 | tf_op jit(solution)/shard_map/reduce_scatter | solution.py:204
  872.9 7.6 fusion.55
  880.6 96.3 %all-gather.27.cloned.1.call-done = bf16[2560,1280]{1,0:T(8,128)(2,1)} async-done(((bf16[320,1280]{1,0:T(8,128)(2,1)}), bf16[2560,1280]{1,0:T(8,128)(2,1)}) %all-gather.27.cloned.1.call-update) | async-done | bytes 6553616 | tf_op jit(solution)/shard_map/all_gather | solution.py:221
  982.4 7.8 fusion.56
  990.3 6.6 fusion.46
  996.9 42.7 %all-reduce = (f32[1280]{0:T(1024)}, f32[1280]{0:T(1024)}, f32[1280]{0:T(1024)}, f32[1280]{0:T(1024)}, f32[80]{0:T(128)}) all-reduce(f32[1280]{0:T(1024)S(1)} %copy-done.34, f32[1280]{0:T(1024)S(1)} %convert_reduce_fusion, f32[1280]{0:T(1024)S(1)} %get-tuple-element.144, ...), channel_id=1, replica_groups=mesh['rep'=8,'fsdp'=2,'ctx'=2] {'rep','fsdp','ctx'}, use_global_device_ids=true, to_apply=%region_24.25 | all-reduce | flops 5200 | bytes 41600 | tf_op jit(solution)/shard_map/psum | solution.py:230
  1039.6 5.9 fusion.43
  1045.5 88.8 %all-reduce.4.cloned.1.call-done = (bf16[320,1280]{1,0:T(8,128)(2,1)}, bf16[320,1280]{1,0:T(8,128)(2,1)}, bf16[320,1280]{1,0:T(8,128)(2,1)}, bf16[320,1280]{1,0:T(8,128)(2,1)}, bf16[320,1280]{1,0:T(8,128)(2,1)}) async-done(((bf16[320,1280]{1,0:T(8,128)(2,1)}, bf16[320,1280]{1,0:T(8,128)(2,1)}, bf16[320,1280]{1,0:T(8,128)(2,1)}, bf16[320,1280]{1,0:T(8,128)(2,1)}, bf16[320,1280]{1,0:T(8,128)(2,1)}), ...) | async-done | bytes 4096016 | tf_op jit(solution)/shard_map/psum | solution.py:224
  (210 shorter events, 87.7 us)
Async XLA Ops:
  7.2 5.2 copy-start.3
  7.2 34.4 %all-gather.17.cloned.1.call-start = ((), (), s32[]{:S(2)}) async-start(), calls=%async_computation.11 | async-start | bytes 4096000 | tf_op jit(solution)/shard_map/all_gather | solution.py:55
  7.9 64.5 %all-gather.11.cloned.1.call-start = ((), (), s32[]{:S(2)}) async-start(), calls=%async_computation.8 | async-start | bytes 4096000 | tf_op jit(solution)/shard_map/all_gather | solution.py:56
  8.7 94.6 %all-gather.15.cloned.1.call-start = ((), (), s32[]{:S(2)}) async-start(), calls=%async_computation.10 | async-start | bytes 4096000 | tf_op jit(solution)/shard_map/all_gather | solution.py:54
  9.4 110.5 %all-gather.19.cloned.1.call-start = ((), (), s32[]{:S(2)}) async-start(), calls=%async_computation.12 | async-start | bytes 7864320 | tf_op jit(solution)/shard_map/all_gather | solution.py:80
  53.9 84.4 %all-gather.13.cloned.1.call-start = ((), (), s32[]{:S(2)}) async-start(), calls=%async_computation.9 | async-start | bytes 7864320 | tf_op jit(solution)/shard_map/all_gather | solution.py:81
  80.2 6.9 copy-start.44
  80.2 6.9 copy-start.26
  84.7 165.9 %all-gather.21.cloned.1.call-start = ((), (), s32[]{:S(2)}) async-start(), calls=%async_computation.13 | async-start | bytes 4096000 | tf_op jit(solution)/shard_map/all_gather | solution.py:57
  85.3 175.0 %all-gather.23.cloned.1.call-start = ((), (), s32[]{:S(2)}) async-start(), calls=%async_computation.14 | async-start | bytes 4096000 | tf_op jit(solution)/shard_map/all_gather | solution.py:58
  86.1 183.7 %all-gather.25.cloned.1.call-start = ((), (), s32[]{:S(2)}) async-start(), calls=%async_computation.15 | async-start | bytes 4096000 | tf_op jit(solution)/shard_map/all_gather | solution.py:59
  86.8 541.3 %reduce-scatter.11.cloned.1.call-start = ((), (), s32[]{:S(2)}) async-start(), calls=%async_computation.17 | async-start | bytes 15728640 | tf_op jit(solution)/shard_map/reduce_scatter | solution.py:175
  87.1 21.8 %copy-start.36 = (f32[80]{0:T(128)}, f32[80]{0:T(128)S(1)}, u32[]{:S(2)}) copy-start(f32[80]{0:T(128)S(1)} %fusion.51) | copy-start | bytes 964
  108.9 31.2 %copy-start.43 = (s32[2]{0:T(128)S(1)}, s32[2]{0:T(128)}, u32[]{:S(2)}) copy-start(s32[2]{0:T(128)} %param.19) | copy-start | bytes 28
  159.9 15.4 %copy-start.5 = (bf16[1,1024,1280]{1,2,0:T(8,128)(2,1)S(1)}, bf16[1,1024,1280]{1,2,0:T(8,128)(2,1)}, u32[]{:S(2)}) copy-start(bf16[1,1024,1280]{1,2,0:T(8,128)(2,1)} %get-tuple-element.329) | copy-start | bytes 7864324 | tf_op jit(solution)/shard_map/while
  159.9 15.4 %copy-start.8 = (bf16[2,512,16,80]{1,3,2,0:T(8,128)(2,1)S(1)}, bf16[2,512,16,80]{1,3,2,0:T(8,128)(2,1)}, u32[]{:S(2)}) copy-start(bf16[2,512,16,80]{1,3,2,0:T(8,128)(2,1)} %get-tuple-element.358) | copy-start | bytes 7864324 | tf_op jit(solution)/shard_map/while
  212.6 15.4 %copy-start.5 = (bf16[1,1024,1280]{1,2,0:T(8,128)(2,1)S(1)}, bf16[1,1024,1280]{1,2,0:T(8,128)(2,1)}, u32[]{:S(2)}) copy-start(bf16[1,1024,1280]{1,2,0:T(8,128)(2,1)} %get-tuple-element.329) | copy-start | bytes 7864324 | tf_op jit(solution)/shard_map/while
  212.6 15.4 %copy-start.8 = (bf16[2,512,16,80]{1,3,2,0:T(8,128)(2,1)S(1)}, bf16[2,512,16,80]{1,3,2,0:T(8,128)(2,1)}, u32[]{:S(2)}) copy-start(bf16[2,512,16,80]{1,3,2,0:T(8,128)(2,1)} %get-tuple-element.358) | copy-start | bytes 7864324 | tf_op jit(solution)/shard_map/while
  250.6 9.8 copy-start.32
  260.3 24.0 %copy-start.30 = (f32[1024]{0:T(1024)}, f32[1024]{0:T(1024)S(1)}, u32[]{:S(2)}) copy-start(f32[1024]{0:T(1024)S(1)} %get-tuple-element.205) | copy-start | bytes 12292
  260.4 9.4 copy-start.41
  269.8 10.1 copy-start.7
  269.8 10.1 copy-start.39
  279.8 4.5 copy-start.46
  279.8 4.5 copy-start.12
  284.3 4.3 copy-start.16
  311.2 6.5 copy-start
  311.2 6.4 copy-start.2
  438.3 8.8 copy-start.1
  447.1 6.4 copy-start
  447.1 6.4 copy-start.2
  574.1 8.8 copy-start.1
  583.3 54.4 %reduce-scatter.9.cloned.1.call-start = ((), (), s32[]{:S(2)}) async-start(), calls=%async_computation.16 | async-start | bytes 15728640 | tf_op jit(solution)/shard_map/reduce_scatter | solution.py:174
  583.9 83.0 %reduce-scatter.13.cloned.1.call-start = ((), (), s32[]{:S(2)}) async-start(), calls=%async_computation.18 | async-start | bytes 4096000 | tf_op jit(solution)/shard_map/reduce_scatter | solution.py:201
  588.9 4.9 copy-start.18
  593.8 5.2 copy-start.13
  593.8 5.2 copy-start.42
  599.0 10.3 copy-start.31
  599.0 10.3 copy-start.33
  599.0 109.1 %reduce-scatter.23.cloned.1.call-start = ((), (), s32[]{:S(2)}) async-start(), calls=%async_computation.23 | async-start | bytes 4096000 | tf_op jit(solution)/shard_map/reduce_scatter | solution.py:216
  609.0 10.2 copy-start.10
  609.0 140.3 %reduce-scatter.21.cloned.1.call-start = ((), (), s32[]{:S(2)}) async-start(), calls=%async_computation.22 | async-start | bytes 4096000 | tf_op jit(solution)/shard_map/reduce_scatter | solution.py:213
  619.2 171.4 %reduce-scatter.19.cloned.1.call-start = ((), (), s32[]{:S(2)}) async-start(), calls=%async_computation.21 | async-start | bytes 4096000 | tf_op jit(solution)/shard_map/reduce_scatter | solution.py:210
  628.0 4.5 copy-start.19
  628.1 203.7 %reduce-scatter.17.cloned.1.call-start = ((), (), s32[]{:S(2)}) async-start(), calls=%async_computation.20 | async-start | bytes 4096000 | tf_op jit(solution)/shard_map/reduce_scatter | solution.py:207
  637.6 235.3 %reduce-scatter.15.cloned.1.call-start = ((), (), s32[]{:S(2)}) async-start(), calls=%async_computation.19 | async-start | bytes 4096000 | tf_op jit(solution)/shard_map/reduce_scatter | solution.py:204
  642.0 25.2 %copy-start.29 = (f32[1,4,2,128]{3,1,2,0:T(4,128)S(1)}, f32[1,4,2,128]{3,1,2,0:T(4,128)}, u32[]{:S(2)}) copy-start(f32[1,4,2,128]{3,1,2,0:T(4,128)} %copy-done.28) | copy-start | bytes 12292
  647.2 20.1 %copy-start.14 = (bf16[2,512,1280]{2,1,0:T(8,128)(2,1)S(1)}, bf16[2,512,1280]{2,1,0:T(8,128)(2,1)}, u32[]{:S(2)}) copy-start(bf16[2,512,1280]{2,1,0:T(8,128)(2,1)} %param.31) | copy-start | bytes 7864324
  647.2 20.5 %copy-start.45 = (f32[80]{0:T(128)S(1)}, f32[80]{0:T(128)}, u32[]{:S(2)}) copy-start(f32[80]{0:T(128)} %param.30) | copy-start | bytes 964
  647.2 20.5 %copy-start.40 = (f32[1280]{0:T(1024)S(1)}, f32[1280]{0:T(1024)}, u32[]{:S(2)}) copy-start(f32[1280]{0:T(1024)} %param.27) | copy-start | bytes 15364
  647.2 329.7 %all-gather.27.cloned.1.call-start = ((), (), s32[]{:S(2)}) async-start(), calls=%async_computation.24 | async-start | bytes 7372800 | tf_op jit(solution)/shard_map/all_gather | solution.py:221
  666.9 467.4 %all-reduce.4.cloned.1.call-start = ((), (), s32[]{:S(2)}) async-start(), calls=%async_computation.25 | async-start | bytes 8192000 | tf_op jit(solution)/shard_map/psum | solution.py:224
  667.7 205.3 %copy-start.15 = (bf16[1280,1280]{1,0:T(8,128)(2,1)S(1)}, bf16[1280,1280]{1,0:T(8,128)(2,1)}, u32[]{:S(2)}) copy-start(bf16[1280,1280]{1,0:T(8,128)(2,1)} %all-gather.15.cloned.1.call-done) | copy-start | bytes 9830404
  981.1 9.1 slice-start
  982.4 7.9 copy-start.4
  982.4 7.9 copy-start.21
  982.4 7.9 copy-start.27
  982.4 7.9 copy-start.38
  982.4 7.9 slice-start.1
  990.3 6.6 copy-start.34
  990.3 6.6 copy-start.35
  1134.3 5.0 copy-start.25
  1134.3 6.3 copy-start.24
  1134.3 7.5 copy-start.23
  (9 other events, 13.9 us)
Sparse Core Ops, SparseCore 0:
  9.6 31.9 all-gather.16
  43.1 29.2 all-gather.10
  74.0 29.2 all-gather.14
  104.7 15.2 all-gather.18
  121.9 16.3 all-gather.12
  139.7 30.4 all-gather.20
  171.7 29.2 all-gather.22
  202.6 29.2 all-gather.24
  583.5 19.2 reduce-scatter.10
  604.9 19.2 reduce-scatter.8
  626.9 40.0 reduce-scatter.12
  669.3 38.6 reduce-scatter.22
  710.6 38.7 reduce-scatter.20
  751.8 38.7 reduce-scatter.18
  793.0 38.7 reduce-scatter.16
  834.2 38.6 reduce-scatter.14
  874.9 101.8 all-gather.26
  981.0 153.2 all-reduce.3
